TPU v7x, 512 devices: a whole 4x4x16 slice. The times are simulated.
512 devices in a mesh: row: 32 (over z, y_lo), col: 16 (over x, y_hi, core).
Axes of the slice: x: 4, y: 4 (y_hi: 2, y_lo: 2; y = y_hi * 2 + y_lo), z: 16, core: 2. Of those that a mesh axis runs over, the one named last changes fastest.
Arguments:
- covariance: float32 [12288, 12288], P('col', 'row'), as said below
- courant_x: float32 [8, 96, 128], replicated, may hold values from -0.4 to 0.4
- courant_y: float32 [8, 96, 128], replicated, may hold values from -0.4 to 0.4
- wind_index: int32 [4], replicated, may hold values from 0 to 7
Outputs:
- forecast: float32 [12288, 12288], P(('row', 'col'))
Inputs may be any that keep to these rules, and one draw needn't show every extreme that they name: covariance is exactly symmetric.
All inputs are finite; a program needn't handle non-finite values.
Results may differ from a plain program's by a relative error of at most 0.00002.
Values sent between devices are 32-bit elements; how exact they have to be, the bound alone decides.
No kernel may reach another device: no remote copies, remote signals or barrier semaphores. Data moves between devices by JAX's collectives and lax.ppermute only.
A program may use at most 64 MiB of HBM per device.

v0:
```python
import jax
import jax.numpy as jnp
from jax import lax
from jax.sharding import PartitionSpec as P

NLAT = 96
NLON = 128


diffusivity = 0.05


def advance(states, flow_east, flow_north):
    eastern = jnp.roll(states, -1, axis=2)
    western = jnp.roll(states, 1, axis=2)
    zeros_row = jnp.zeros_like(states[:, :1, :])
    northern = jnp.concatenate([states[:, 1:, :], zeros_row], axis=1)
    southern = jnp.concatenate([zeros_row, states[:, :-1, :]], axis=1)
    upwind = jnp.maximum(flow_east, 0.0) * (states - western) + jnp.minimum(flow_east, 0.0) * (
        eastern - states
    )
    upwind = (
        upwind
        + jnp.maximum(flow_north, 0.0) * (states - southern)
        + jnp.minimum(flow_north, 0.0) * (northern - states)
    )
    return states - upwind + diffusivity * (eastern + western + northern + southern - 4.0 * states)


def propagate(states, courant_x, courant_y, wind_index):

    def advance_once(counter, current):
        chosen = wind_index[counter]
        flow_east = lax.dynamic_index_in_dim(courant_x, chosen, 0, keepdims=False)
        flow_north = lax.dynamic_index_in_dim(courant_y, chosen, 0, keepdims=False)
        return advance(current, flow_east, flow_north)

    return lax.fori_loop(0, wind_index.shape[0], advance_once, states)


def shards(covariance, courant_x, courant_y, wind_index):
    row_count = lax.axis_size("row")
    col_count = lax.axis_size("col")
    cells_all = NLAT * NLON
    columns_dev = cells_all // (row_count * col_count)
    blocks = covariance.T.reshape(col_count, columns_dev, covariance.shape[0])
    pieces = lax.all_to_all(blocks, "col", split_axis=0, concat_axis=2, tiled=True)
    items = pieces.shape[1]
    states = pieces.reshape(items, NLAT, NLON)
    propagated = propagate(states, courant_x, courant_y, wind_index).reshape(1, items, cells_all)
    propagated = propagated.reshape(columns_dev, cells_all)
    regrouped = lax.all_to_all(
        lax.all_to_all(propagated, "row", split_axis=1, concat_axis=0, tiled=True),
        "col",
        split_axis=1,
        concat_axis=0,
        tiled=True,
    )
    regrouped = regrouped.reshape(col_count, row_count, columns_dev, columns_dev)
    regrouped = regrouped.transpose(1, 0, 2, 3).reshape(cells_all, columns_dev)
    crossed = regrouped.T.reshape(columns_dev, NLAT, NLON)
    return propagate(crossed, courant_x, courant_y, wind_index).reshape(columns_dev, cells_all)


def solution(mesh):
    placed = (P("col", "row"), P(), P(), P())
    return jax.shard_map(
        shards, mesh=mesh, in_specs=placed, out_specs=P(("row", "col"), None), check_vma=False
    )
```

profile of v0, /device:TPU:1, one launch (start us, length us, event | category | flops | bytes accessed | tf_op | source)
XLA Modules:
  0.0 214.3 jit_solution(4192107874986851114)
XLA Ops:
  0.0 2.7 %copy.15 = f32[768,384]{0,1:T(8,128)} copy(f32[768,384]{1,0:T(8,128)} %param.8) | data formatting | bytes 2359296 | tf_op args[0]
  2.7 10.3 %all-to-all-start = ((f32[16,24,768]{2,1,0:T(8,128)}), f32[16,24,768]{2,1,0:T(8,128)S(1)}, u32[]{:S(2)}, u32[]{:S(2)}) async-start(f32[16,24,768]{2,1,0:T(8,128)} %bitcast.11), calls=%async_computation | async-start | bytes 2359296 | tf_op jit(solution)/shard_map/all_to_all | solution.py:47
  13.0 18.6 %all-to-all-done = f32[16,24,768]{2,1,0:T(8,128)S(1)} async-done(((f32[16,24,768]{2,1,0:T(8,128)}), f32[16,24,768]{2,1,0:T(8,128)S(1)}, u32[]{:S(2)}, u32[]{:S(2)}) %all-to-all-start) | async-done | bytes 1179680 | tf_op jit(solution)/shard_map/all_to_all | solution.py:47
  32.6 23.3 %while.26 = (s32[]{:T(128)}, f32[24,96,128]{2,1,0:T(8,128)S(1)}, s32[4]{0:T(128)S(1)}, f32[8,96,128]{2,1,0:T(8,128)}, f32[8,96,128]{2,1,0:T(8,128)}, /*index=5*/s32[]{:T(128)}, s32[]{:T(128)}, s32[]{:T(128)}) while((s32[]{:T(128)}, f32[24,96,128]{2,1,0:T(8,128)S(1)}, s32[4]{0:T(128)S(1)}, f32[8,96,128]{2,1,0:T(8,128)}, ...), condition=%wide.region_1.2_spmd, body=%wide.region_0.1_spmd.sunk | while | flops 6242309 | bytes 16933000 | solution.py:38
  35.1 0.8 maximum_bitcast_fusion.6
  37.0 1.3 multiply_add_fusion.4
  38.4 0.6 dynamic_slice.56
  40.9 0.8 maximum_bitcast_fusion.6
  42.9 1.3 multiply_add_fusion.4
  46.8 0.8 maximum_bitcast_fusion.6
  48.7 1.3 multiply_add_fusion.4
  52.6 0.8 maximum_bitcast_fusion.6
  54.5 1.3 multiply_add_fusion.4
  56.1 0.7 copy.17
  56.8 73.3 %all_to_all.47 = f32[24,32,384]{2,0,1:T(8,128)S(1)} all-to-all(f32[24,32,384]{2,0,1:T(8,128)S(1)} %copy.17), channel_id=1, replica_groups=mesh['row'=32,'col'=16] {'row'}, dimensions={1} | all-to-all | bytes 2359296 | tf_op jit(solution)/shard_map/all_to_all | solution.py:53
  130.1 5.3 %all_to_all.41 = f32[768,16,24]{2,1,0:T(8,128)} reshape(f32[32,24,384]{2,1,0:T(8,128)S(1)} %bitcast.54) | data formatting | bytes 2359296 | tf_op jit(solution)/shard_map/all_to_all | solution.py:52
  135.4 6.0 %copy.18 = f32[768,16,24]{0,2,1:T(8,128)} copy(f32[768,16,24]{2,1,0:T(8,128)} %all_to_all.41) | data formatting | bytes 2359296 | tf_op jit(solution)/shard_map/all_to_all | solution.py:52
  141.4 6.8 %all-to-all-start.2 = ((f32[768,16,24]{0,2,1:T(8,128)}), f32[768,16,24]{0,2,1:T(8,128)S(1)}, u32[]{:S(2)}, u32[]{:S(2)}) async-start(f32[768,16,24]{0,2,1:T(8,128)} %copy.18), calls=%async_computation.2 | async-start | bytes 2359296 | tf_op jit(solution)/shard_map/all_to_all | solution.py:52
  148.2 18.5 %all-to-all-done.2 = f32[768,16,24]{0,2,1:T(8,128)S(1)} async-done(((f32[768,16,24]{0,2,1:T(8,128)}), f32[768,16,24]{0,2,1:T(8,128)S(1)}, u32[]{:S(2)}, u32[]{:S(2)}) %all-to-all-start.2) | async-done | bytes 1179680 | tf_op jit(solution)/shard_map/all_to_all | solution.py:52
  166.7 5.9 %reshape.30 = f32[16,32,24,24]{2,1,3,0:T(8,128)} reshape(f32[16,768,24]{1,2,0:T(8,128)S(1)} %bitcast.53) | data formatting | bytes 2359296 | tf_op jit(solution)/shard_map/reshape | solution.py:59
  172.6 10.8 %copy.19 = f32[32,16,24,24]{2,1,0,3:T(8,128)} copy(f32[32,16,24,24]{2,0,3,1:T(8,128)} %bitcast.52) | data formatting | bytes 2359296 | tf_op jit(solution)/shard_map/transpose | solution.py:60
  183.4 5.7 %reshape.31 = f32[12288,24]{0,1:T(8,128)S(1)} reshape(f32[32,16,24,24]{2,1,0,3:T(8,128)} %copy.19) | data formatting | bytes 2359296 | tf_op jit(solution)/shard_map/reshape | solution.py:60
  189.3 23.3 %while.27 = (s32[]{:T(128)}, f32[24,96,128]{2,1,0:T(8,128)S(1)}, s32[4]{0:T(128)S(1)}, f32[8,96,128]{2,1,0:T(8,128)}, f32[8,96,128]{2,1,0:T(8,128)}, /*index=5*/s32[]{:T(128)}, s32[]{:T(128)}, s32[]{:T(128)}) while((s32[]{:T(128)}, f32[24,96,128]{2,1,0:T(8,128)S(1)}, s32[4]{0:T(128)S(1)}, f32[8,96,128]{2,1,0:T(8,128)}, ...), condition=%wide.region_3.4_spmd, body=%wide.region_2.3_spmd.sunk | while | flops 6242309 | bytes 16933000 | solution.py:38
  191.9 0.8 maximum_bitcast_fusion.7
  193.8 1.3 multiply_add_fusion.5
  197.7 0.8 maximum_bitcast_fusion.7
  199.6 1.3 multiply_add_fusion.5
  203.5 0.8 maximum_bitcast_fusion.7
  205.4 1.3 multiply_add_fusion.5
  209.3 0.8 maximum_bitcast_fusion.7
  211.3 1.3 multiply_add_fusion.5
  212.6 1.7 copy.23
  (37 shorter events, 14.0 us)
Async XLA Ops:
  2.7 28.9 %all-to-all-start = ((f32[16,24,768]{2,1,0:T(8,128)}), f32[16,24,768]{2,1,0:T(8,128)S(1)}, u32[]{:S(2)}, u32[]{:S(2)}) async-start(f32[16,24,768]{2,1,0:T(8,128)} %bitcast.11), calls=%async_computation | async-start | bytes 2359296 | tf_op jit(solution)/shard_map/all_to_all | solution.py:47
  31.9 0.7 copy-start
  141.4 25.3 %all-to-all-start.2 = ((f32[768,16,24]{0,2,1:T(8,128)}), f32[768,16,24]{0,2,1:T(8,128)S(1)}, u32[]{:S(2)}, u32[]{:S(2)}) async-start(f32[768,16,24]{0,2,1:T(8,128)} %copy.18), calls=%async_computation.2 | async-start | bytes 2359296 | tf_op jit(solution)/shard_map/all_to_all | solution.py:52
where the time goes:
time: 215 us; the launch traced here: 214 us
  blocking collectives  73.3 us (34%)
  local copies, waits for them, and re-layouts  53.4 us (25%)
  waiting for transfers between devices  37.1 us (17%)
  other arithmetic  17.5 us (8%)
  starting transfers between devices  17.1 us (8%)
  loops' own time  15.9 us (7%)
    all_to_all x1, blocking collectives, shards(): lax.all_to_all(propagated, 'row', split_axis=1, concat_axis=0, tiled=True)  73.3 us
    all_to_all x1, waiting for transfers between devices, shards(): lax.all_to_all(blocks, 'col', split_axis=0, concat_axis=2, tiled=True)  18.6 us
    all_to_all x1, waiting for transfers between devices, shards(): lax.all_to_all(lax.all_to_all(propagated, 'row', split_axis=1, concat_axi...  18.5 us
    another operation x2, loops' own time, propagate(): return lax.fori_loop(0, wind_index.shape[0], advance_once, states)  15.9 us
    all_to_all x2, local copies, waits for them, and re-layouts, shards(): lax.all_to_all(lax.all_to_all(propagated, 'row', split_axis=1, concat_axi...  11.3 us
    transpose x1, local copies, waits for them, and re-layouts, shards(): regrouped = regrouped.transpose(1, 0, 2, 3).reshape(cells_all, columns_dev)  10.8 us
    add x8, other arithmetic, advance(): states - upwind  10.8 us
    all_to_all x1, starting transfers between devices, shards(): lax.all_to_all(blocks, 'col', split_axis=0, concat_axis=2, tiled=True)  10.3 us
  transfers between devices with their start and end apart: 2, of which 2 were waited for; matrix products, arithmetic and copies ran while one was open for 0% of the time, Pallas kernels for 0%

commit v1 on v0

v1 whole, which is shorter than its diff:
```python
import functools

import jax
import jax.numpy as jnp
from jax import lax
from jax.experimental import pallas as pl
from jax.experimental.pallas import tpu as pltpu
from jax.sharding import Mesh, PartitionSpec as P

NLAT = 96
NLON = 128
STEPS = 4
HALO = STEPS
DIFFUSIVITY = 0.05
LATS_DEV = 3
LATS_PLANE = 2 * LATS_DEV
WINDOW = LATS_PLANE + 2 * HALO


def coef_kernel(wind_ref, cx_ref, cy_ref, out_ref):
    flow_east = cx_ref[0]
    flow_north = cy_ref[0]
    east_pos = jnp.maximum(flow_east, 0.0)
    east_neg = jnp.minimum(flow_east, 0.0)
    north_pos = jnp.maximum(flow_north, 0.0)
    north_neg = jnp.minimum(flow_north, 0.0)
    centre = 1.0 - 4.0 * DIFFUSIVITY - (east_pos - east_neg) - (north_pos - north_neg)
    parts = (
        centre,
        east_pos + DIFFUSIVITY,
        DIFFUSIVITY - east_neg,
        north_pos + DIFFUSIVITY,
        DIFFUSIVITY - north_neg,
    )
    out_ref[...] = jnp.zeros_like(out_ref)
    for k, part in enumerate(parts):
        out_ref[0, pl.ds(8 * HALO + k, NLAT, stride=8), :] = part


def coefficients(courant_x, courant_y, wind_index):
    rows = 8 * (NLAT + 2 * HALO)
    out = pl.pallas_call(
        coef_kernel,
        grid_spec=pltpu.PrefetchScalarGridSpec(
            num_scalar_prefetch=1,
            grid=(STEPS,),
            in_specs=[
                pl.BlockSpec((1, NLAT, NLON), lambda s, wind: (wind[s], 0, 0)),
                pl.BlockSpec((1, NLAT, NLON), lambda s, wind: (wind[s], 0, 0)),
            ],
            out_specs=pl.BlockSpec((1, rows, NLON), lambda s, wind: (s, 0, 0)),
        ),
        out_shape=jax.ShapeDtypeStruct((STEPS, rows, NLON), jnp.float32),
        compiler_params=pltpu.CompilerParams(vmem_limit_bytes=24 << 20),
        name="coefs",
    )(wind_index, courant_x, courant_y)
    return out.reshape(STEPS, NLAT + 2 * HALO, 8, NLON)


def stencil(coef, x, south, north):
    west = pltpu.roll(x, 1, 1)
    east = pltpu.roll(x, NLON - 1, 1)
    return (
        x * coef[0:1]
        + west * coef[1:2]
        + east * coef[2:3]
        + (south * coef[3:4] + north * coef[4:5])
    )


def left_kernel(place_ref, coef_ref, own, pair, big1, small1, big2, small2, out_ref, w0, w1):
    z = place_ref[0]
    yl = place_ref[1]
    for i in range(LATS_DEV):
        lanes = slice(i * NLON, (i + 1) * NLON)
        w0[HALO + LATS_DEV * yl + i] = own[:, lanes]
        w0[HALO + LATS_DEV - LATS_DEV * yl + i] = pair[:, lanes]
        w0[10 - 9 * yl + i] = big1[:, lanes]
        w0[1 + 9 * yl + i] = big2[:, lanes]
    w0[13 * yl] = small1[...]
    w0[13 - 13 * yl] = small2[...]
    bufs = (w0, w1)
    for s in range(STEPS):
        src, dst = bufs[s % 2], bufs[(s + 1) % 2]

        def body(p, carry, s=s, src=src, dst=dst):
            coef = coef_ref[s, LATS_PLANE * z + p]
            new = stencil(coef, src[p], src[p - 1], src[p + 1])
            if s == STEPS - 1:
                out_ref[pl.ds(pl.multiple_of((p - HALO) * NLON, NLON), NLON), :] = new.T
            else:
                dst[p] = new
            return carry

        lax.fori_loop(s + 1, WINDOW - 1 - s, body, 0)


def right_kernel(coef_ref, got_ref, out_ref, b0, b1):
    rows = out_ref.shape[0]
    half = got_ref.shape[0] // 2
    zero = jnp.zeros((rows, NLON), jnp.float32)
    for buf in (b0, b1):
        buf[0] = zero
        buf[NLAT + 1] = zero

    def gather(c, carry):
        for yl in range(2):
            for i in range(LATS_DEV):
                b0[1 + c * LATS_PLANE + yl * LATS_DEV + i] = got_ref[
                    yl * half + c, :, i * NLON : (i + 1) * NLON
                ]
        return carry

    lax.fori_loop(0, half, gather, 0)
    bufs = (b0, b1)
    unroll = 8
    for s in range(STEPS):
        src, dst = bufs[s % 2], bufs[(s + 1) % 2]

        def body(j, carry, s=s, src=src, dst=dst):
            for i in range(unroll):
                lat = j * unroll + i
                new = stencil(coef_ref[s, lat + HALO], src[lat + 1], src[lat], src[lat + 2])
                if s == STEPS - 1:
                    out_ref[:, pl.ds(pl.multiple_of(lat * NLON, NLON), NLON)] = new
                else:
                    dst[lat + 1] = new
            return carry

        lax.fori_loop(0, NLAT // unroll, body, 0)


def shards(covariance, courant_x, courant_y, wind_index):
    planes = lax.axis_size("z")
    yl = lax.axis_index("yl")
    z = lax.axis_index("z")
    place = jnp.stack([z, yl]).astype(jnp.int32)
    cols = covariance.shape[0] // 2
    row = ("z", "yl")
    swap = [(r, r ^ 1) for r in range(2 * planes)]
    outward = [(r, r + (2 if r % 2 else -2)) for r in range(2 * planes)]
    outward = [(a, b) for a, b in outward if 0 <= b < 2 * planes]
    inward = [(b, a) for a, b in outward]

    other = lax.dynamic_slice_in_dim(covariance, (1 - yl) * cols, cols, 0)
    own = lax.dynamic_slice_in_dim(covariance, yl * cols, cols, 0)
    pair = lax.ppermute(other, row, swap)
    big1 = lax.ppermute(own, row, outward)
    small1 = lax.ppermute(
        lax.dynamic_slice_in_dim(own, (1 - yl) * 2 * NLON, NLON, 1), row, inward
    )
    big2 = lax.ppermute(pair, row, inward)
    small2 = lax.ppermute(lax.dynamic_slice_in_dim(pair, yl * 2 * NLON, NLON, 1), row, outward)

    coefs = coefficients(courant_x, courant_y, wind_index)

    window = pltpu.VMEM((WINDOW, cols, NLON), jnp.float32)
    vmem = pl.BlockSpec(memory_space=pltpu.VMEM)
    propagated = pl.pallas_call(
        left_kernel,
        in_specs=[pl.BlockSpec(memory_space=pltpu.SMEM)] + [vmem] * 7,
        out_specs=vmem,
        out_shape=jax.ShapeDtypeStruct((LATS_PLANE * NLON, cols), jnp.float32),
        scratch_shapes=[window, window],
        compiler_params=pltpu.CompilerParams(vmem_limit_bytes=24 << 20),
        name="left",
    )(place, coefs, own, pair, big1, small1, big2, small2)

    group = ("yl", "x", "yh", "core")
    members = 2 * lax.axis_size("x") * lax.axis_size("yh") * lax.axis_size("core")
    rows_dev = propagated.shape[0] // members
    sent = propagated.reshape(members, rows_dev, cols)
    got = lax.all_to_all(sent, group, split_axis=0, concat_axis=0, tiled=True)

    state = pltpu.VMEM((NLAT + 2, rows_dev, NLON), jnp.float32)
    return pl.pallas_call(
        right_kernel,
        in_specs=[vmem, vmem],
        out_specs=vmem,
        out_shape=jax.ShapeDtypeStruct((rows_dev, NLAT * NLON), jnp.float32),
        scratch_shapes=[state, state],
        compiler_params=pltpu.CompilerParams(vmem_limit_bytes=24 << 20),
        name="right",
    )(coefs, got)


def solution(mesh):
    inner = Mesh(mesh.devices.reshape(16, 2, 4, 2, 2), ("z", "yl", "x", "yh", "core"))
    row, col = ("z", "yl"), ("x", "yh", "core")
    placed = (P(col, row), P(), P(), P())
    return jax.shard_map(
        shards, mesh=inner, in_specs=placed, out_specs=P(row + col, None), check_vma=False
    )
```

time: 215 us -> 80.9 us (0.38)
  local copies, waits for them, and re-layouts: 53.4 us -> 3.83 us
  blocking collectives: 73.3 us -> 28.5 us
  waiting for transfers between devices: 37.1 us -> 14 us
  other arithmetic: 17.5 us -> 0.08 us
  loops' own time: 15.9 us -> 0 us
  Pallas kernels: 0 us -> 15.3 us
    all_to_all x1, blocking collectives: 73.3 us -> 28.5 us  [shards(): got = lax.all_to_all(sent, group, split_axis=0, concat_axis=0, tiled=True)]
    all_to_all x2 -> x0, waiting for transfers between devices: 37.1 us -> none  [the longest x1 18.6 us: shards(): lax.all_to_all(blocks, 'col', split_axis=0, concat_axis=2, tiled=True)]
    ppermute x0 -> x5, starting transfers between devices: none -> 18.3 us  [the longest x1 8.24 us: shards(): big2 = lax.ppermute(pair, row, inward)]
    all_to_all x2 -> x0, starting transfers between devices: 17.1 us -> none  [the longest x1 10.3 us: shards(): lax.all_to_all(blocks, 'col', split_axis=0, concat_axis=2, tiled=True)]
    another operation x2 -> x0, loops' own time: 15.9 us -> none  [propagate(): return lax.fori_loop(0, wind_index.shape[0], advance_once, states)]
    pallas_call x0 -> x3, Pallas kernels: none -> 15.3 us  [the longest x1 7.38 us: shards(): pl.pallas_call(left_kernel, in_specs=[pl.BlockSpec(memory_space=pltpu.SME...]
    ppermute x0 -> x5, waiting for transfers between devices: none -> 14 us  [the longest x1 7.12 us: shards(): lax.ppermute(lax.dynamic_slice_in_dim(own, (1 - yl) * 2 * NLON, NLON, 1),...]
    all_to_all x5 -> x0, local copies, waits for them, and re-layouts: 12.6 us -> none  [the longest x2 11.3 us: shards(): lax.all_to_all(lax.all_to_all(propagated, 'row', split_axis=1, concat_axi...]
  transfers between devices with their start and end apart: 2 -> 5, of which waited for: 2 -> 2; matrix products, arithmetic and copies ran while one was open for 0% -> 3% of each run, Pallas kernels for 0% -> 1%
where the time goes in v1:
time: 80.9 us; the launch traced here: 80.2 us
  blocking collectives  28.5 us (35%)
  starting transfers between devices  18.3 us (23%)
  Pallas kernels  15.3 us (19%)
  waiting for transfers between devices  14 us (17%)
  local copies, waits for them, and re-layouts  3.83 us (5%)
    all_to_all x1, blocking collectives, shards(): got = lax.all_to_all(sent, group, split_axis=0, concat_axis=0, tiled=True)  28.5 us
    ppermute x1, starting transfers between devices, shards(): big2 = lax.ppermute(pair, row, inward)  8.24 us
    pallas_call x1, Pallas kernels, shards(): pl.pallas_call(left_kernel, in_specs=[pl.BlockSpec(memory_space=pltpu.SME...  7.38 us
    ppermute x1, waiting for transfers between devices, shards(): lax.ppermute(lax.dynamic_slice_in_dim(own, (1 - yl) * 2 * NLON, NLON, 1),...  7.12 us
    pallas_call x1, Pallas kernels, shards(): pl.pallas_call(right_kernel, in_specs=[vmem, vmem], out_specs=vmem, out_s...  6.97 us
    ppermute x1, waiting for transfers between devices, shards(): pair = lax.ppermute(other, row, swap)  6.92 us
    ppermute x1, starting transfers between devices, shards(): pair = lax.ppermute(other, row, swap)  4.02 us
    ppermute x1, starting transfers between devices, shards(): lax.ppermute(lax.dynamic_slice_in_dim(own, (1 - yl) * 2 * NLON, NLON, 1),...  3.51 us
  transfers between devices with their start and end apart: 5, of which 2 were waited for; matrix products, arithmetic and copies ran while one was open for 3% of the time, Pallas kernels for 1%

profile of v1, /device:TPU:1, one launch (start us, length us, event | category | flops | bytes accessed | tf_op | source)
XLA Modules:
  0.0 80.2 jit_solution(1305791905840222731)
XLA Ops:
  0.0 0.0 copy-start
  0.0 0.0 copy-start.1
  0.0 0.0 copy-start.2
  0.0 1.4 %constant_dynamic-slice_fusion.1 = (f32[384,384]{1,0:T(8,128)S(1)}, f32[384,384]{1,0:T(8,128)S(1)}) fusion(f32[768,384]{1,0:T(8,128)} %param.4, s32[]{:T(128)S(6)} %select_n.17, s32[]{:T(128)S(6)} %select_n.16), kind=kLoop, calls=%fused_computation.1 | loop fusion | bytes 2359304 | tf_op jit(solution)/shard_map/dynamic_slice | solution.py:145
  1.4 4.0 %collective-permute-start = (f32[384,384]{1,0:T(8,128)S(1)}, f32[384,384]{1,0:T(8,128)S(1)}, u32[]{:S(2)}, u32[]{:S(2)}) collective-permute-start(f32[384,384]{1,0:T(8,128)S(1)} %get-tuple-element.5), channel_id=1, source_target_pairs={{0,16},{16,0},{32,48},{48,32},{64,80},{80,64},{96,112},{112,96},{1... | collective-permute-start | bytes 1769480 | tf_op jit(solution)/shard_map/ppermute | solution.py:147
  5.4 1.3 %collective-permute-start.1 = (f32[384,384]{1,0:T(8,128)S(1)}, f32[384,384]{1,0:T(8,128)S(1)}, u32[]{:S(2)}, u32[]{:S(2)}) collective-permute-start(f32[384,384]{1,0:T(8,128)S(1)} %get-tuple-element.6.own), channel_id=1, source_target_pairs={{16,48},{32,0},{48,80},{64,32},{80,112},{96,64},{112,144},{128,96}... | collective-permute-start | bytes 1769480 | tf_op jit(solution)/shard_map/ppermute | solution.py:148
  6.7 6.9 %collective-permute-done.pair = f32[384,384]{1,0:T(8,128)S(1)} collective-permute-done((f32[384,384]{1,0:T(8,128)S(1)}, f32[384,384]{1,0:T(8,128)S(1)}, u32[]{:S(2)}, u32[]{:S(2)}) %collective-permute-start) | collective-permute-done | bytes 589856 | tf_op jit(solution)/shard_map/ppermute | solution.py:147
  13.7 8.2 %collective-permute-start.3 = (f32[384,384]{1,0:T(8,128)S(1)}, f32[384,384]{1,0:T(8,128)S(1)}, u32[]{:S(2)}, u32[]{:S(2)}) collective-permute-start(f32[384,384]{1,0:T(8,128)S(1)} %collective-permute-done.pair), channel_id=1, source_target_pairs={{48,16},{0,32},{80,48},{32,64},{112,80},{64,96},{144,112},{96,128}... | collective-permute-start | bytes 1769480 | tf_op jit(solution)/shard_map/ppermute | solution.py:152
  21.9 1.7 %dynamic_slice.14 = f32[384,128]{1,0:T(8,128)} dynamic-slice(f32[768,384]{1,0:T(8,128)} %param.4, s32[]{:T(128)S(6)} %select_n.18, s32[]{:T(128)S(6)} %select_n.20), dynamic_slice_sizes={384,128} | dynamic-slice | bytes 393220 | tf_op jit(solution)/shard_map/dynamic_slice | solution.py:150
  23.7 3.5 %collective-permute-start.2 = (f32[384,128]{1,0:T(8,128)}, f32[384,128]{1,0:T(8,128)S(1)}, u32[]{:S(2)}, u32[]{:S(2)}) collective-permute-start(f32[384,128]{1,0:T(8,128)} %dynamic_slice.14), channel_id=1, source_target_pairs={{48,16},{0,32},{80,48},{32,64},{112,80},{64,96},{144,112},{96,128}... | collective-permute-start | bytes 589832 | tf_op jit(solution)/shard_map/ppermute | solution.py:149
  27.2 0.7 constant_dynamic-slice_fusion
  27.9 1.3 %collective-permute-start.4 = (f32[384,128]{1,0:T(8,128)}, f32[384,128]{1,0:T(8,128)S(1)}, u32[]{:S(2)}, u32[]{:S(2)}) collective-permute-start(f32[384,128]{1,0:T(8,128)} %constant_dynamic-slice_fusion), channel_id=1, source_target_pairs={{16,48},{32,0},{48,80},{64,32},{80,112},{96,64},{112,144},{128,96}... | collective-permute-start | bytes 589832 | tf_op jit(solution)/shard_map/ppermute | solution.py:153
  29.2 0.0 copy-done
  29.2 0.0 copy-done.1
  29.2 0.0 copy-done.2
  29.2 0.9 %coefs.1 = f32[4,832,128]{2,1,0:T(8,128)S(1)} custom-call(s32[4]{0:T(128)S(1)} %copy-done.2, f32[8,96,128]{2,1,0:T(8,128)S(1)} %copy-done, f32[8,96,128]{2,1,0:T(8,128)S(1)} %copy-done.1), custom_call_target="tpu_custom_call" | custom-call | tf_op jit(solution)/shard_map/coefs/pallas_call | solution.py:42
  30.1 0.1 pad_add_fusion.place_ref
  30.2 7.1 %collective-permute-done.2.small1 = f32[384,128]{1,0:T(8,128)S(1)} collective-permute-done((f32[384,128]{1,0:T(8,128)}, f32[384,128]{1,0:T(8,128)S(1)}, u32[]{:S(2)}, u32[]{:S(2)}) %collective-permute-start.2) | collective-permute-done | bytes 196640 | tf_op jit(solution)/shard_map/ppermute | solution.py:149
  37.3 0.0 collective-permute-done.1.big1
  37.3 0.0 collective-permute-done.4.small2
  37.3 0.0 collective-permute-done.3.big2
  37.3 7.4 %left.1 = f32[768,384]{1,0:T(8,128)S(1)} custom-call(s32[2]{0:T(128)S(1)} %pad_add_fusion.place_ref, f32[4,104,8,128]{3,2,1,0:T(8,128)S(1)} %bitcast.4, f32[384,384]{1,0:T(8,128)S(1)} %get-tuple-element.6.own, f32[384,384]{1,0:T(8,128)S(1)} %collective-permute-done.pair, f32[384,384]{1,0:T(8,128)S(1)} %collective-permute-done.1.big1, ...), custom_call_target="tpu_custom_call" | custom-call | tf_op jit(solution)/shard_map/left/pallas_call | solution.py:159
  44.7 28.5 %all_to_all.5.got_ref = f32[32,24,384]{2,1,0:T(8,128)S(1)} all-to-all(f32[32,24,384]{2,1,0:T(8,128)S(1)} %bitcast.6), channel_id=1, replica_groups=mesh['z'=16,'yl'=2,'x'=4,'yh'=2,'core'=2] {'yl','x','yh','core'}, dimensions={0} | all-to-all | bytes 2359296 | tf_op jit(solution)/shard_map/all_to_all | solution.py:173
  73.2 7.0 %right.1 = f32[24,12288]{1,0:T(8,128)} custom-call(f32[4,104,8,128]{3,2,1,0:T(8,128)S(1)} %bitcast.5, f32[32,24,384]{2,1,0:T(8,128)S(1)} %all_to_all.5.got_ref), custom_call_target="tpu_custom_call" | custom-call | tf_op jit(solution)/shard_map/right/pallas_call | solution.py:176
Async XLA Ops:
  0.0 29.2 %copy-start = (f32[8,96,128]{2,1,0:T(8,128)S(1)}, f32[8,96,128]{2,1,0:T(8,128)}, u32[]{:S(2)}) copy-start(f32[8,96,128]{2,1,0:T(8,128)} %cx_ref.1) | copy-start | bytes 1179652
  0.0 29.2 %copy-start.1 = (f32[8,96,128]{2,1,0:T(8,128)S(1)}, f32[8,96,128]{2,1,0:T(8,128)}, u32[]{:S(2)}) copy-start(f32[8,96,128]{2,1,0:T(8,128)} %cy_ref.1) | copy-start | bytes 1179652
  0.0 29.2 %copy-start.2 = (s32[4]{0:T(128)S(1)}, s32[4]{0:T(128)}, u32[]{:S(2)}) copy-start(s32[4]{0:T(128)} %wind_ref.1) | copy-start | bytes 52
  1.4 12.2 %collective-permute-start = (f32[384,384]{1,0:T(8,128)S(1)}, f32[384,384]{1,0:T(8,128)S(1)}, u32[]{:S(2)}, u32[]{:S(2)}) collective-permute-start(f32[384,384]{1,0:T(8,128)S(1)} %get-tuple-element.5), channel_id=1, source_target_pairs={{0,16},{16,0},{32,48},{48,32},{64,80},{80,64},{96,112},{112,96},{1... | collective-permute-start | bytes 1769480 | tf_op jit(solution)/shard_map/ppermute | solution.py:147
  5.4 31.9 %collective-permute-start.1 = (f32[384,384]{1,0:T(8,128)S(1)}, f32[384,384]{1,0:T(8,128)S(1)}, u32[]{:S(2)}, u32[]{:S(2)}) collective-permute-start(f32[384,384]{1,0:T(8,128)S(1)} %get-tuple-element.6.own), channel_id=1, source_target_pairs={{16,48},{32,0},{48,80},{64,32},{80,112},{96,64},{112,144},{128,96}... | collective-permute-start | bytes 1769480 | tf_op jit(solution)/shard_map/ppermute | solution.py:148
  13.7 23.7 %collective-permute-start.3 = (f32[384,384]{1,0:T(8,128)S(1)}, f32[384,384]{1,0:T(8,128)S(1)}, u32[]{:S(2)}, u32[]{:S(2)}) collective-permute-start(f32[384,384]{1,0:T(8,128)S(1)} %collective-permute-done.pair), channel_id=1, source_target_pairs={{48,16},{0,32},{80,48},{32,64},{112,80},{64,96},{144,112},{96,128}... | collective-permute-start | bytes 1769480 | tf_op jit(solution)/shard_map/ppermute | solution.py:152
  23.7 13.7 %collective-permute-start.2 = (f32[384,128]{1,0:T(8,128)}, f32[384,128]{1,0:T(8,128)S(1)}, u32[]{:S(2)}, u32[]{:S(2)}) collective-permute-start(f32[384,128]{1,0:T(8,128)} %dynamic_slice.14), channel_id=1, source_target_pairs={{48,16},{0,32},{80,48},{32,64},{112,80},{64,96},{144,112},{96,128}... | collective-permute-start | bytes 589832 | tf_op jit(solution)/shard_map/ppermute | solution.py:149
  27.9 9.5 %collective-permute-start.4 = (f32[384,128]{1,0:T(8,128)}, f32[384,128]{1,0:T(8,128)S(1)}, u32[]{:S(2)}, u32[]{:S(2)}) collective-permute-start(f32[384,128]{1,0:T(8,128)} %constant_dynamic-slice_fusion), channel_id=1, source_target_pairs={{16,48},{32,0},{48,80},{64,32},{80,112},{96,64},{112,144},{128,96}... | collective-permute-start | bytes 589832 | tf_op jit(solution)/shard_map/ppermute | solution.py:153

commit v2 on v1

v2 whole, which is shorter than its diff:
```python
import jax
import jax.numpy as jnp
from jax import lax
from jax.experimental import pallas as pl
from jax.experimental.pallas import tpu as pltpu
from jax.sharding import Mesh, PartitionSpec as P


NLAT = 96
NLON = 128
STEPS = 4
HALO = STEPS
DIFFUSIVITY = 0.05
LATS_DEV = 3
LATS_PLANE = 2 * LATS_DEV
WINDOW = LATS_PLANE + 2 * HALO
PARTS = (192, 192)
VMEM_LIMIT = 24 << 20


def coef_kernel(wind_ref, cx_ref, cy_ref, out_ref):
    flow_east = cx_ref[0]
    flow_north = cy_ref[0]
    east_pos = jnp.maximum(flow_east, 0.0)
    east_neg = jnp.minimum(flow_east, 0.0)
    north_pos = jnp.maximum(flow_north, 0.0)
    north_neg = jnp.minimum(flow_north, 0.0)
    centre = 1.0 - 4.0 * DIFFUSIVITY - (east_pos - east_neg) - (north_pos - north_neg)
    parts = (
        centre,
        east_pos + DIFFUSIVITY,
        DIFFUSIVITY - east_neg,
        north_pos + DIFFUSIVITY,
        DIFFUSIVITY - north_neg,
    )
    out_ref[...] = jnp.zeros_like(out_ref)
    for k, part in enumerate(parts):
        out_ref[0, pl.ds(8 * HALO + k, NLAT, stride=8), :] = part


def coefficients(courant_x, courant_y, wind_index):
    rows = 8 * (NLAT + 2 * HALO)
    out = pl.pallas_call(
        coef_kernel,
        grid_spec=pltpu.PrefetchScalarGridSpec(
            num_scalar_prefetch=1,
            grid=(STEPS,),
            in_specs=[
                pl.BlockSpec((1, NLAT, NLON), lambda s, wind: (wind[s], 0, 0)),
                pl.BlockSpec((1, NLAT, NLON), lambda s, wind: (wind[s], 0, 0)),
            ],
            out_specs=pl.BlockSpec((1, rows, NLON), lambda s, wind: (s, 0, 0)),
        ),
        out_shape=jax.ShapeDtypeStruct((STEPS, rows, NLON), jnp.float32),
        compiler_params=pltpu.CompilerParams(vmem_limit_bytes=VMEM_LIMIT),
        name="coefs",
    )(wind_index, courant_x, courant_y)
    return out.reshape(STEPS, NLAT + 2 * HALO, 8, NLON)


def stencil(coef, x, south, north):
    west = pltpu.roll(x, 1, 1)
    east = pltpu.roll(x, NLON - 1, 1)
    return (
        x * coef[0:1]
        + west * coef[1:2]
        + east * coef[2:3]
        + (south * coef[3:4] + north * coef[4:5])
    )


def lanes_of(yl, j):
    i = LATS_DEV - 1 - j + yl * (2 * j - LATS_DEV + 1)
    return pl.ds(pl.multiple_of(i * NLON, NLON), NLON)


def place_of(yl, q):
    return WINDOW - 1 - q + yl * (2 * q - WINDOW + 1)


def mirrored(coef_ref, place_ref, s, q, x, before, after):
    z = place_ref[0]
    yl = place_ref[1]
    lat = LATS_PLANE * z + place_of(yl, q)
    west = pltpu.roll(x, 1, 1)
    east = pltpu.roll(x, NLON - 1, 1)
    return (
        x * coef_ref[s, lat, 0:1, :]
        + west * coef_ref[s, lat, 1:2, :]
        + east * coef_ref[s, lat, 2:3, :]
        + (
            before * coef_ref[s, lat, pl.ds(4 - yl, 1), :]
            + after * coef_ref[s, lat, pl.ds(3 + yl, 1), :]
        )
    )


EARLY = [(s, q) for s in range(1, STEPS + 1) for q in range(1 + s, 10 - s)]
LATE = [(s, q) for s in range(1, STEPS + 1) for q in [s, *range(10 - s, 14 - s)]]


def early_kernel(place_ref, coef_ref, own, out1, *refs):
    *pairs, kept, done = refs
    yl = place_ref[1]

    def load(s, q):
        if s:
            return kept[EARLY.index((s, q))]
        if q < 4:
            return out1[:, lanes_of(yl, q - 1)]
        if q < 7:
            return jnp.concatenate([pair[:, lanes_of(yl, q - 4)] for pair in pairs], axis=0)
        return own[:, lanes_of(yl, q - 7)]

    for n, (s, q) in enumerate(EARLY):
        x, before, after = load(s - 1, q), load(s - 1, q - 1), load(s - 1, q + 1)
        new = mirrored(coef_ref, place_ref, s - 1, q, x, before, after)
        if s == STEPS:
            done[...] = new.T
        else:
            kept[n] = new


def late_kernel(place_ref, coef_ref, own, out1, in1, out2, kept, done, *refs):
    *in2, out_ref, state = refs
    yl = place_ref[1]

    def rows_of(q):
        first = (place_of(yl, q) - HALO) * NLON
        return pl.ds(pl.multiple_of(first, NLON), NLON)

    def load(s, q):
        if (s, q) in LATE:
            return state[LATE.index((s, q))]
        if s:
            return kept[EARLY.index((s, q))]
        if q == 0:
            return out2[...]
        if q == WINDOW - 1:
            return in1[...]
        if q < 4:
            return out1[:, lanes_of(yl, q - 1)]
        if q < 10:
            return own[:, lanes_of(yl, q - 7)]
        return jnp.concatenate([part[:, lanes_of(yl, q - 10)] for part in in2], axis=0)

    out_ref[rows_of(EARLY[-1][1]), :] = done[...]
    for n, (s, q) in enumerate(LATE):
        x, before, after = load(s - 1, q), load(s - 1, q - 1), load(s - 1, q + 1)
        new = mirrored(coef_ref, place_ref, s - 1, q, x, before, after)
        if s == STEPS:
            out_ref[rows_of(q), :] = new.T
        else:
            state[n] = new


def cut_kernel(place_ref, cov_ref, own, near, *refs):
    *others, sems = refs
    yl = place_ref[1]
    cols = own.shape[0]
    mine = pl.ds(pl.multiple_of(yl * cols, cols), cols)
    inner = pl.ds(pl.multiple_of((1 - yl) * 2 * NLON, NLON), NLON)
    copies = []
    base = 0
    for n, other in enumerate(others):
        size = other.shape[0]
        theirs = pl.ds(pl.multiple_of((1 - yl) * cols + base, 8), size)
        copies.append(pltpu.make_async_copy(cov_ref.at[theirs, :], other, sems.at[2 + n]))
        base += size
    copies.append(pltpu.make_async_copy(cov_ref.at[mine, :], own, sems.at[0]))
    copies.append(pltpu.make_async_copy(cov_ref.at[mine, inner], near, sems.at[1]))
    for copy in copies:
        copy.start()
    for copy in copies:
        copy.wait()


def right_kernel(coef_ref, got_ref, out_ref, b0, b1, result, sems):
    half = got_ref.shape[0] // 2
    chunks = sems.shape[0]
    each = NLAT // chunks

    def first(lat):
        c, rest = divmod(lat, LATS_PLANE)
        yl, i = divmod(rest, LATS_DEV)
        return got_ref[yl * half + c, :, i * NLON : (i + 1) * NLON]

    zero = jnp.zeros((out_ref.shape[0], NLON), jnp.float32)
    bufs = (b0, b1)
    copies = []
    for s in range(STEPS):
        dst = bufs[(s + 1) % 2]
        load = first if s == 0 else lambda lat, src=bufs[s % 2]: src[lat]
        for lat in range(NLAT):
            south = load(lat - 1) if lat > 0 else zero
            north = load(lat + 1) if lat < NLAT - 1 else zero
            new = stencil(coef_ref[s, lat + HALO], load(lat), south, north)
            if s < STEPS - 1:
                dst[lat] = new
                continue
            result[:, lat * NLON : (lat + 1) * NLON] = new
            if (lat + 1) % each == 0:
                n = lat // each
                span = slice(n * each * NLON, (n + 1) * each * NLON)
                copy = pltpu.make_async_copy(result.at[:, span], out_ref.at[:, span], sems.at[n])
                copy.start()
                copies.append(copy)
    for copy in copies:
        copy.wait()


def shards(covariance, courant_x, courant_y, wind_index):
    planes = lax.axis_size("z")
    yl = lax.axis_index("yl")
    z = lax.axis_index("z")
    place = jnp.stack([z, yl]).astype(jnp.int32)
    cols = covariance.shape[0] // 2
    row = ("z", "yl")
    swap = [(r, r ^ 1) for r in range(2 * planes)]
    outward = [(r, r + (2 if r % 2 else -2)) for r in range(2 * planes)]
    outward = [(a, b) for a, b in outward if 0 <= b < 2 * planes]
    inward = [(b, a) for a, b in outward]
    smem = pl.BlockSpec(memory_space=pltpu.SMEM)
    vmem = pl.BlockSpec(memory_space=pltpu.VMEM)

    def shape(*dims):
        return jax.ShapeDtypeStruct(dims, jnp.float32)

    params = pltpu.CompilerParams(vmem_limit_bytes=VMEM_LIMIT)

    own, near, *others = pl.pallas_call(
        cut_kernel,
        in_specs=[smem, pl.BlockSpec(memory_space=pltpu.HBM)],
        out_specs=[vmem] * (2 + len(PARTS)),
        out_shape=[shape(cols, LATS_DEV * NLON), shape(cols, NLON)]
        + [shape(size, LATS_DEV * NLON) for size in PARTS],
        scratch_shapes=[pltpu.SemaphoreType.DMA((2 + len(PARTS),))],
        compiler_params=params,
        name="cut",
    )(place, covariance)
    pairs, in2 = [], []
    for other in others:
        pairs.append(lax.ppermute(other, row, swap))
    in1 = lax.ppermute(near, row, inward)
    out1 = lax.ppermute(own, row, outward)
    for pair in pairs:
        in2.append(lax.ppermute(pair, row, inward))
    far = [lax.dynamic_slice_in_dim(pair, yl * 2 * NLON, NLON, 1) for pair in pairs]
    out2 = lax.ppermute(jnp.concatenate(far, axis=0), row, outward)

    coefs = coefficients(courant_x, courant_y, wind_index)

    kept, done = pl.pallas_call(
        early_kernel,
        in_specs=[smem] + [vmem] * (3 + len(pairs)),
        out_specs=[vmem, vmem],
        out_shape=[shape(len(EARLY) - 1, cols, NLON), shape(NLON, cols)],
        compiler_params=params,
        name="early",
    )(place, coefs, own, out1, *pairs)
    propagated = pl.pallas_call(
        late_kernel,
        in_specs=[smem] + [vmem] * (7 + len(in2)),
        out_specs=vmem,
        out_shape=shape(LATS_PLANE * NLON, cols),
        scratch_shapes=[pltpu.VMEM((len(LATE) - 5, cols, NLON), jnp.float32)],
        compiler_params=params,
        name="late",
    )(place, coefs, own, out1, in1, out2, kept, done, *in2)

    group = ("yl", "x", "yh", "core")
    members = 2 * lax.axis_size("x") * lax.axis_size("yh") * lax.axis_size("core")
    rows_dev = LATS_PLANE * NLON // members
    sent = propagated.reshape(members, rows_dev, cols)
    got = lax.all_to_all(sent, group, split_axis=0, concat_axis=0, tiled=True)

    state = pltpu.VMEM((NLAT, rows_dev, NLON), jnp.float32)
    return pl.pallas_call(
        right_kernel,
        in_specs=[vmem, vmem],
        out_specs=pl.BlockSpec(memory_space=pl.ANY),
        out_shape=jax.ShapeDtypeStruct((rows_dev, NLAT * NLON), jnp.float32),
        scratch_shapes=[
            state,
            state,
            pltpu.VMEM((rows_dev, NLAT * NLON), jnp.float32),
            pltpu.SemaphoreType.DMA((4,)),
        ],
        compiler_params=pltpu.CompilerParams(vmem_limit_bytes=VMEM_LIMIT),
        name="right",
    )(coefs, got)


def solution(mesh):
    inner = Mesh(mesh.devices.reshape(16, 2, 4, 2, 2), ("z", "yl", "x", "yh", "core"))
    row, col = ("z", "yl"), ("x", "yh", "core")
    placed = (P(col, row), P(), P(), P())
    return jax.shard_map(
        shards, mesh=inner, in_specs=placed, out_specs=P(row + col, None), check_vma=False
    )
```

time: 80.9 us -> 68 us (0.84)
  the two profiles are of different devices: /device:TPU:1 before, /device:TPU:225 now
where the time goes in v2:
time: 68 us; the launch traced here: 67.7 us
  blocking collectives  30 us (44%)
  starting transfers between devices  22 us (32%)
  Pallas kernels  11.2 us (16%)
  waiting for transfers between devices  2.97 us (4%)
  local copies, waits for them, and re-layouts  1.31 us (2%)
    all_to_all x1, blocking collectives, shards(): got = lax.all_to_all(sent, group, split_axis=0, concat_axis=0, tiled=True)  30 us
    ppermute x2, starting transfers between devices, shards(): in2.append(lax.ppermute(pair, row, inward))  8.11 us
    ppermute x2, starting transfers between devices, shards(): pairs.append(lax.ppermute(other, row, swap))  5.28 us
    ppermute x1, starting transfers between devices, shards(): in1 = lax.ppermute(near, row, inward)  4.76 us
    pallas_call x1, Pallas kernels, shards(): pl.pallas_call(right_kernel, in_specs=[vmem, vmem], out_specs=pl.BlockSpe...  3.53 us
    pallas_call x1, Pallas kernels, shards(): pl.pallas_call(late_kernel, in_specs=[smem] + [vmem] * (7 + len(in2)), ou...  3.4 us
    pallas_call x1, Pallas kernels, shards(): pl.pallas_call(early_kernel, in_specs=[smem] + [vmem] * (3 + len(pairs)),...  2.47 us
    ppermute x1, waiting for transfers between devices, shards(): out2 = lax.ppermute(jnp.concatenate(far, axis=0), row, outward)  2.23 us
  transfers between devices with their start and end apart: 7, of which 2 were waited for; matrix products, arithmetic and copies ran while one was open for 0% of the time, Pallas kernels for 5%

profile of v2, /device:TPU:225, one launch (start us, length us, event | category | flops | bytes accessed | tf_op | source)
XLA Modules:
  0.0 67.7 jit_solution(2442115021898512297)
XLA Ops:
  0.0 0.0 copy-start.3
  0.0 0.1 pad_add_fusion.place_ref
  0.1 0.0 copy-start
  0.1 1.3 %copy-done = f32[768,384]{1,0:T(8,128)S(1)} copy-done((f32[768,384]{1,0:T(8,128)S(1)}, f32[768,384]{1,0:T(8,128)}, u32[]{:S(2)}) %copy-start) | copy-done | bytes 1179672
  1.3 0.0 copy-start.1
  1.4 0.0 copy-start.2
  1.4 0.8 %cut.1 = (f32[384,384]{1,0:T(8,128)S(1)}, f32[384,128]{1,0:T(8,128)S(1)}, f32[192,384]{1,0:T(8,128)S(1)}, f32[192,384]{1,0:T(8,128)S(1)}) custom-call(s32[2]{0:T(128)S(1)} %pad_add_fusion.place_ref, f32[768,384]{1,0:T(8,128)S(1)} %copy-done), custom_call_target="tpu_custom_call" | custom-call | tf_op jit(solution)/shard_map/cut/pallas_call | solution.py:231
  2.2 3.2 %collective-permute-start.2 = (f32[192,384]{1,0:T(8,128)S(1)}, f32[192,384]{1,0:T(8,128)S(1)}, u32[]{:S(2)}, u32[]{:S(2)}) collective-permute-start(f32[192,384]{1,0:T(8,128)S(1)} %get-tuple-element.13), channel_id=1, source_target_pairs={{0,16},{16,0},{32,48},{48,32},{64,80},{80,64},{96,112},{112,96},{1... | collective-permute-start | bytes 884744 | tf_op jit(solution)/shard_map/ppermute | solution.py:243
  5.4 2.1 %collective-permute-start.3 = (f32[192,384]{1,0:T(8,128)S(1)}, f32[192,384]{1,0:T(8,128)S(1)}, u32[]{:S(2)}, u32[]{:S(2)}) collective-permute-start(f32[192,384]{1,0:T(8,128)S(1)} %get-tuple-element.14), channel_id=1, source_target_pairs={{0,16},{16,0},{32,48},{48,32},{64,80},{80,64},{96,112},{112,96},{1... | collective-permute-start | bytes 884744 | tf_op jit(solution)/shard_map/ppermute | solution.py:243
  7.5 1.9 %collective-permute-start = (f32[384,384]{1,0:T(8,128)S(1)}, f32[384,384]{1,0:T(8,128)S(1)}, u32[]{:S(2)}, u32[]{:S(2)}) collective-permute-start(f32[384,384]{1,0:T(8,128)S(1)} %get-tuple-element.11.own), channel_id=1, source_target_pairs={{16,48},{32,0},{48,80},{64,32},{80,112},{96,64},{112,144},{128,96}... | collective-permute-start | bytes 1769480 | tf_op jit(solution)/shard_map/ppermute | solution.py:245
  9.4 4.8 %collective-permute-start.1 = (f32[384,128]{1,0:T(8,128)S(1)}, f32[384,128]{1,0:T(8,128)S(1)}, u32[]{:S(2)}, u32[]{:S(2)}) collective-permute-start(f32[384,128]{1,0:T(8,128)S(1)} %get-tuple-element.12), channel_id=1, source_target_pairs={{48,16},{0,32},{80,48},{32,64},{112,80},{64,96},{144,112},{96,128}... | collective-permute-start | bytes 589832 | tf_op jit(solution)/shard_map/ppermute | solution.py:244
  14.2 0.0 collective-permute-done.2.refs_0_
  14.2 3.4 %collective-permute-start.5 = (f32[192,384]{1,0:T(8,128)S(1)}, f32[192,384]{1,0:T(8,128)S(1)}, u32[]{:S(2)}, u32[]{:S(2)}) collective-permute-start(f32[192,384]{1,0:T(8,128)S(1)} %collective-permute-done.2.refs_0_), channel_id=1, source_target_pairs={{48,16},{0,32},{80,48},{32,64},{112,80},{64,96},{144,112},{96,128}... | collective-permute-start | bytes 884744 | tf_op jit(solution)/shard_map/ppermute | solution.py:247
  17.6 0.7 %collective-permute-done.3.refs_1_ = f32[192,384]{1,0:T(8,128)S(1)} collective-permute-done((f32[192,384]{1,0:T(8,128)S(1)}, f32[192,384]{1,0:T(8,128)S(1)}, u32[]{:S(2)}, u32[]{:S(2)}) %collective-permute-start.3) | collective-permute-done | bytes 294944 | tf_op jit(solution)/shard_map/ppermute | solution.py:243
  18.3 4.7 %collective-permute-start.6 = (f32[192,384]{1,0:T(8,128)S(1)}, f32[192,384]{1,0:T(8,128)S(1)}, u32[]{:S(2)}, u32[]{:S(2)}) collective-permute-start(f32[192,384]{1,0:T(8,128)S(1)} %collective-permute-done.3.refs_1_), channel_id=1, source_target_pairs={{48,16},{0,32},{80,48},{32,64},{112,80},{64,96},{144,112},{96,128}... | collective-permute-start | bytes 884744 | tf_op jit(solution)/shard_map/ppermute | solution.py:247
  23.1 1.9 %collective-permute-start.4 = (f32[384,128]{1,0:T(8,128)S(1)}, f32[384,128]{1,0:T(8,128)S(1)}, u32[]{:S(2)}, u32[]{:S(2)}) collective-permute-start(f32[384,128]{1,0:T(8,128)S(1)} %pad_maximum_fusion), channel_id=1, source_target_pairs={{16,48},{32,0},{48,80},{64,32},{80,112},{96,64},{112,144},{128,96}... | collective-permute-start | bytes 589832 | tf_op jit(solution)/shard_map/ppermute | solution.py:249
  25.1 0.0 copy-done.3
  25.1 0.0 copy-done.1
  25.1 0.0 copy-done.2
  25.1 0.9 %coefs.1 = f32[4,832,128]{2,1,0:T(8,128)S(1)} custom-call(s32[4]{0:T(128)S(1)} %copy-done.3, f32[8,96,128]{2,1,0:T(8,128)S(1)} %copy-done.1, f32[8,96,128]{2,1,0:T(8,128)S(1)} %copy-done.2), custom_call_target="tpu_custom_call" | custom-call | tf_op jit(solution)/shard_map/coefs/pallas_call | solution.py:43
  26.0 0.0 collective-permute-done.out1
  26.1 2.5 %early.1 = (f32[15,384,128]{2,1,0:T(8,128)S(1)}, f32[128,384]{1,0:T(8,128)S(1)}) custom-call(s32[2]{0:T(128)S(1)} %pad_add_fusion.place_ref, f32[4,104,8,128]{3,2,1,0:T(8,128)S(1)} %bitcast.4, f32[384,384]{1,0:T(8,128)S(1)} %get-tuple-element.11.own, f32[384,384]{1,0:T(8,128)S(1)} %collective-permute-done.out1, ...), custom_call_target="tpu_custom_call" | custom-call | tf_op jit(solution)/shard_map/early/pallas_call | solution.py:253
  28.5 0.0 collective-permute-done.1.in1
  28.5 2.2 %collective-permute-done.4.out2 = f32[384,128]{1,0:T(8,128)S(1)} collective-permute-done((f32[384,128]{1,0:T(8,128)S(1)}, f32[384,128]{1,0:T(8,128)S(1)}, u32[]{:S(2)}, u32[]{:S(2)}) %collective-permute-start.4) | collective-permute-done | bytes 196640 | tf_op jit(solution)/shard_map/ppermute | solution.py:249
  30.8 0.0 collective-permute-done.5.refs_0_
  30.8 0.0 collective-permute-done.6.refs_1_
  30.8 3.4 %late.1 = f32[768,384]{1,0:T(8,128)S(1)} custom-call(s32[2]{0:T(128)S(1)} %pad_add_fusion.place_ref, f32[4,104,8,128]{3,2,1,0:T(8,128)S(1)} %bitcast.5, f32[384,384]{1,0:T(8,128)S(1)} %get-tuple-element.11.own, f32[384,384]{1,0:T(8,128)S(1)} %collective-permute-done.out1, f32[384,128]{1,0:T(8,128)S(1)} %collective-permute-done.1.in1, ...), custom_call_target="tpu_custom_call" | custom-call | tf_op jit(solution)/shard_map/late/pallas_call | solution.py:261
  34.2 30.0 %all_to_all.5.got_ref = f32[32,24,384]{2,1,0:T(8,128)S(1)} all-to-all(f32[32,24,384]{2,1,0:T(8,128)S(1)} %bitcast.7), channel_id=1, replica_groups=mesh['z'=16,'yl'=2,'x'=4,'yh'=2,'core'=2] {'yl','x','yh','core'}, dimensions={0} | all-to-all | bytes 2359296 | tf_op jit(solution)/shard_map/all_to_all | solution.py:275
  64.2 3.5 %right.1 = f32[24,12288]{1,0:T(8,128)} custom-call(f32[4,104,8,128]{3,2,1,0:T(8,128)S(1)} %bitcast.6, f32[32,24,384]{2,1,0:T(8,128)S(1)} %all_to_all.5.got_ref), custom_call_target="tpu_custom_call" | custom-call | tf_op jit(solution)/shard_map/right/pallas_call | solution.py:278
  (3 shorter events, 0.0 us)
Async XLA Ops:
  0.0 25.1 %copy-start.3 = (s32[4]{0:T(128)S(1)}, s32[4]{0:T(128)}, u32[]{:S(2)}) copy-start(s32[4]{0:T(128)} %wind_ref.1) | copy-start | bytes 52
  0.1 1.3 %copy-start = (f32[768,384]{1,0:T(8,128)S(1)}, f32[768,384]{1,0:T(8,128)}, u32[]{:S(2)}) copy-start(f32[768,384]{1,0:T(8,128)} %cov_ref.1) | copy-start | bytes 3538948
  1.3 23.7 %copy-start.1 = (f32[8,96,128]{2,1,0:T(8,128)S(1)}, f32[8,96,128]{2,1,0:T(8,128)}, u32[]{:S(2)}) copy-start(f32[8,96,128]{2,1,0:T(8,128)} %cx_ref.1) | copy-start | bytes 1179652
  1.4 23.7 %copy-start.2 = (f32[8,96,128]{2,1,0:T(8,128)S(1)}, f32[8,96,128]{2,1,0:T(8,128)}, u32[]{:S(2)}) copy-start(f32[8,96,128]{2,1,0:T(8,128)} %cy_ref.1) | copy-start | bytes 1179652
  2.2 12.0 %collective-permute-start.2 = (f32[192,384]{1,0:T(8,128)S(1)}, f32[192,384]{1,0:T(8,128)S(1)}, u32[]{:S(2)}, u32[]{:S(2)}) collective-permute-start(f32[192,384]{1,0:T(8,128)S(1)} %get-tuple-element.13), channel_id=1, source_target_pairs={{0,16},{16,0},{32,48},{48,32},{64,80},{80,64},{96,112},{112,96},{1... | collective-permute-start | bytes 884744 | tf_op jit(solution)/shard_map/ppermute | solution.py:243
  5.4 12.9 %collective-permute-start.3 = (f32[192,384]{1,0:T(8,128)S(1)}, f32[192,384]{1,0:T(8,128)S(1)}, u32[]{:S(2)}, u32[]{:S(2)}) collective-permute-start(f32[192,384]{1,0:T(8,128)S(1)} %get-tuple-element.14), channel_id=1, source_target_pairs={{0,16},{16,0},{32,48},{48,32},{64,80},{80,64},{96,112},{112,96},{1... | collective-permute-start | bytes 884744 | tf_op jit(solution)/shard_map/ppermute | solution.py:243
  7.5 18.5 %collective-permute-start = (f32[384,384]{1,0:T(8,128)S(1)}, f32[384,384]{1,0:T(8,128)S(1)}, u32[]{:S(2)}, u32[]{:S(2)}) collective-permute-start(f32[384,384]{1,0:T(8,128)S(1)} %get-tuple-element.11.own), channel_id=1, source_target_pairs={{16,48},{32,0},{48,80},{64,32},{80,112},{96,64},{112,144},{128,96}... | collective-permute-start | bytes 1769480 | tf_op jit(solution)/shard_map/ppermute | solution.py:245
  9.4 19.1 %collective-permute-start.1 = (f32[384,128]{1,0:T(8,128)S(1)}, f32[384,128]{1,0:T(8,128)S(1)}, u32[]{:S(2)}, u32[]{:S(2)}) collective-permute-start(f32[384,128]{1,0:T(8,128)S(1)} %get-tuple-element.12), channel_id=1, source_target_pairs={{48,16},{0,32},{80,48},{32,64},{112,80},{64,96},{144,112},{96,128}... | collective-permute-start | bytes 589832 | tf_op jit(solution)/shard_map/ppermute | solution.py:244
  14.2 16.6 %collective-permute-start.5 = (f32[192,384]{1,0:T(8,128)S(1)}, f32[192,384]{1,0:T(8,128)S(1)}, u32[]{:S(2)}, u32[]{:S(2)}) collective-permute-start(f32[192,384]{1,0:T(8,128)S(1)} %collective-permute-done.2.refs_0_), channel_id=1, source_target_pairs={{48,16},{0,32},{80,48},{32,64},{112,80},{64,96},{144,112},{96,128}... | collective-permute-start | bytes 884744 | tf_op jit(solution)/shard_map/ppermute | solution.py:247
  18.3 12.5 %collective-permute-start.6 = (f32[192,384]{1,0:T(8,128)S(1)}, f32[192,384]{1,0:T(8,128)S(1)}, u32[]{:S(2)}, u32[]{:S(2)}) collective-permute-start(f32[192,384]{1,0:T(8,128)S(1)} %collective-permute-done.3.refs_1_), channel_id=1, source_target_pairs={{48,16},{0,32},{80,48},{32,64},{112,80},{64,96},{144,112},{96,128}... | collective-permute-start | bytes 884744 | tf_op jit(solution)/shard_map/ppermute | solution.py:247
  23.1 7.6 %collective-permute-start.4 = (f32[384,128]{1,0:T(8,128)S(1)}, f32[384,128]{1,0:T(8,128)S(1)}, u32[]{:S(2)}, u32[]{:S(2)}) collective-permute-start(f32[384,128]{1,0:T(8,128)S(1)} %pad_maximum_fusion), channel_id=1, source_target_pairs={{16,48},{32,0},{48,80},{64,32},{80,112},{96,64},{112,144},{128,96}... | collective-permute-start | bytes 589832 | tf_op jit(solution)/shard_map/ppermute | solution.py:249

commit v3 on v2

--- a/solution.py
+++ b/solution.py
@@ -1,3 +1,5 @@
+import functools
+
 import jax
 import jax.numpy as jnp
 from jax import lax
@@ -14,7 +16,7 @@
 LATS_DEV = 3
 LATS_PLANE = 2 * LATS_DEV
 WINDOW = LATS_PLANE + 2 * HALO
-PARTS = (192, 192)
+PARTS = (256, 128)
 VMEM_LIMIT = 24 << 20
 
 
@@ -121,9 +123,13 @@
             kept[n] = new
 
 
-def late_kernel(place_ref, coef_ref, own, out1, in1, out2, kept, done, *refs):
-    *in2, out_ref, state = refs
+def late_kernel(base, place_ref, coef_ref, own, out1, in1, out2, in2, kept, done, *refs):
+    *before_refs, out_ref, state = refs
     yl = place_ref[1]
+    size = in2.shape[0]
+    mine = slice(base, base + size)
+    for ref in before_refs:
+        out_ref[:, :base] = ref[...]
 
     def rows_of(q):
         first = (place_of(yl, q) - HALO) * NLON
@@ -133,46 +139,36 @@
         if (s, q) in LATE:
             return state[LATE.index((s, q))]
         if s:
-            return kept[EARLY.index((s, q))]
+            return kept[EARLY.index((s, q)), mine, :]
         if q == 0:
-            return out2[...]
+            return out2[mine, :]
         if q == WINDOW - 1:
-            return in1[...]
+            return in1[mine, :]
         if q < 4:
-            return out1[:, lanes_of(yl, q - 1)]
+            return out1[mine, lanes_of(yl, q - 1)]
         if q < 10:
-            return own[:, lanes_of(yl, q - 7)]
-        return jnp.concatenate([part[:, lanes_of(yl, q - 10)] for part in in2], axis=0)
-
-    out_ref[rows_of(EARLY[-1][1]), :] = done[...]
+            return own[mine, lanes_of(yl, q - 7)]
+        return in2[:, lanes_of(yl, q - 10)]
+
+    out_ref[rows_of(EARLY[-1][1]), mine] = done[:, mine]
     for n, (s, q) in enumerate(LATE):
         x, before, after = load(s - 1, q), load(s - 1, q - 1), load(s - 1, q + 1)
         new = mirrored(coef_ref, place_ref, s - 1, q, x, before, after)
         if s == STEPS:
-            out_ref[rows_of(q), :] = new.T
+            out_ref[rows_of(q), mine] = new.T
         else:
             state[n] = new
 
 
-def cut_kernel(place_ref, cov_ref, own, near, *refs):
-    *others, sems = refs
+def pick_kernel(outer, place_ref, *refs):
+    *pieces, out_ref = refs
     yl = place_ref[1]
-    cols = own.shape[0]
-    mine = pl.ds(pl.multiple_of(yl * cols, cols), cols)
-    inner = pl.ds(pl.multiple_of((1 - yl) * 2 * NLON, NLON), NLON)
-    copies = []
+    i = (LATS_DEV - 1) * (yl if outer else 1 - yl)
+    lanes = pl.ds(pl.multiple_of(i * NLON, NLON), NLON)
     base = 0
-    for n, other in enumerate(others):
-        size = other.shape[0]
-        theirs = pl.ds(pl.multiple_of((1 - yl) * cols + base, 8), size)
-        copies.append(pltpu.make_async_copy(cov_ref.at[theirs, :], other, sems.at[2 + n]))
-        base += size
-    copies.append(pltpu.make_async_copy(cov_ref.at[mine, :], own, sems.at[0]))
-    copies.append(pltpu.make_async_copy(cov_ref.at[mine, inner], near, sems.at[1]))
-    for copy in copies:
-        copy.start()
-    for copy in copies:
-        copy.wait()
+    for piece in pieces:
+        out_ref[base : base + piece.shape[0], :] = piece[:, lanes]
+        base += piece.shape[0]
 
 
 def right_kernel(coef_ref, got_ref, out_ref, b0, b1, result, sems):
@@ -217,8 +213,9 @@
     cols = covariance.shape[0] // 2
     row = ("z", "yl")
     swap = [(r, r ^ 1) for r in range(2 * planes)]
-    outward = [(r, r + (2 if r % 2 else -2)) for r in range(2 * planes)]
-    outward = [(a, b) for a, b in outward if 0 <= b < 2 * planes]
+    devices = 2 * planes
+    outward = [(r, r + (2 if r % 2 else -2)) for r in range(devices)]
+    outward = [(a, b) for a, b in outward if 0 <= b < devices]
     inward = [(b, a) for a, b in outward]
     smem = pl.BlockSpec(memory_space=pltpu.SMEM)
     vmem = pl.BlockSpec(memory_space=pltpu.VMEM)
@@ -228,25 +225,27 @@
 
     params = pltpu.CompilerParams(vmem_limit_bytes=VMEM_LIMIT)
 
-    own, near, *others = pl.pallas_call(
-        cut_kernel,
-        in_specs=[smem, pl.BlockSpec(memory_space=pltpu.HBM)],
-        out_specs=[vmem] * (2 + len(PARTS)),
-        out_shape=[shape(cols, LATS_DEV * NLON), shape(cols, NLON)]
-        + [shape(size, LATS_DEV * NLON) for size in PARTS],
-        scratch_shapes=[pltpu.SemaphoreType.DMA((2 + len(PARTS),))],
-        compiler_params=params,
-        name="cut",
-    )(place, covariance)
+    def pick(outer, *pieces):
+        return pl.pallas_call(
+            functools.partial(pick_kernel, outer),
+            in_specs=[smem] + [vmem] * len(pieces),
+            out_specs=vmem,
+            out_shape=shape(cols, NLON),
+            compiler_params=params,
+            name="pick",
+        )(place, *pieces)
+
+    own = lax.optimization_barrier(lax.dynamic_slice_in_dim(covariance, yl * cols, cols, 0))
     pairs, in2 = [], []
-    for other in others:
+    base = (1 - yl) * cols
+    for k, size in enumerate(PARTS):
+        other = lax.dynamic_slice_in_dim(covariance, base, size, 0)
+        base += size
         pairs.append(lax.ppermute(other, row, swap))
-    in1 = lax.ppermute(near, row, inward)
+        in2.append(lax.ppermute(pairs[k], row, inward))
+    in1 = lax.ppermute(pick(False, own), row, inward)
     out1 = lax.ppermute(own, row, outward)
-    for pair in pairs:
-        in2.append(lax.ppermute(pair, row, inward))
-    far = [lax.dynamic_slice_in_dim(pair, yl * 2 * NLON, NLON, 1) for pair in pairs]
-    out2 = lax.ppermute(jnp.concatenate(far, axis=0), row, outward)
+    out2 = lax.ppermute(pick(True, *pairs), row, outward)
 
     coefs = coefficients(courant_x, courant_y, wind_index)
 
@@ -258,20 +257,25 @@
         compiler_params=params,
         name="early",
     )(place, coefs, own, out1, *pairs)
-    propagated = pl.pallas_call(
-        late_kernel,
-        in_specs=[smem] + [vmem] * (7 + len(in2)),
-        out_specs=vmem,
-        out_shape=shape(LATS_PLANE * NLON, cols),
-        scratch_shapes=[pltpu.VMEM((len(LATE) - 5, cols, NLON), jnp.float32)],
-        compiler_params=params,
-        name="late",
-    )(place, coefs, own, out1, in1, out2, kept, done, *in2)
+    propagated = []
+    base = 0
+    for k, size in enumerate(PARTS):
+        propagated = [
+            pl.pallas_call(
+                functools.partial(late_kernel, base),
+                in_specs=[smem] + [vmem] * (8 + len(propagated)),
+                out_specs=vmem,
+                out_shape=shape(LATS_PLANE * NLON, base + size),
+                scratch_shapes=[pltpu.VMEM((len(LATE) - 5, size, NLON), jnp.float32)],
+                compiler_params=params,
+            )(place, coefs, own, out1, in1, out2, in2[k], kept, done, *propagated)
+        ]
+        base += size
 
     group = ("yl", "x", "yh", "core")
     members = 2 * lax.axis_size("x") * lax.axis_size("yh") * lax.axis_size("core")
     rows_dev = LATS_PLANE * NLON // members
-    sent = propagated.reshape(members, rows_dev, cols)
+    sent = propagated[0].reshape(members, rows_dev, cols)
     got = lax.all_to_all(sent, group, split_axis=0, concat_axis=0, tiled=True)
 
     state = pltpu.VMEM((NLAT, rows_dev, NLON), jnp.float32)
@@ -284,7 +288,7 @@
             state,
             state,
             pltpu.VMEM((rows_dev, NLAT * NLON), jnp.float32),
-            pltpu.SemaphoreType.DMA((4,)),
+            pltpu.SemaphoreType.DMA((8,)),
         ],
         compiler_params=pltpu.CompilerParams(vmem_limit_bytes=VMEM_LIMIT),
         name="right",

time: 68 us -> 71.3 us (1.049)
  the two profiles are of different devices: /device:TPU:225 before, /device:TPU:97 now
where the time goes in v3:
time: 71.3 us; the launch traced here: 70.9 us
  blocking collectives  29.4 us (41%)
  starting transfers between devices  24.9 us (35%)
  Pallas kernels  12.3 us (17%)
  local copies, waits for them, and re-layouts  2.13 us (3%)
  waiting for transfers between devices  1.81 us (3%)
    all_to_all x1, blocking collectives, shards(): got = lax.all_to_all(sent, group, split_axis=0, concat_axis=0, tiled=True)  29.4 us
    ppermute x2, starting transfers between devices, shards(): in2.append(lax.ppermute(pairs[k], row, inward))  9.32 us
    ppermute x2, starting transfers between devices, shards(): pairs.append(lax.ppermute(other, row, swap))  8.11 us
    pallas_call x2, Pallas kernels, shards(): pl.pallas_call(functools.partial(late_kernel, base), in_specs=[smem] + [v...  4.28 us
    ppermute x1, starting transfers between devices, shards(): in1 = lax.ppermute(pick(False, own), row, inward)  3.55 us
    pallas_call x1, Pallas kernels, shards(): pl.pallas_call(right_kernel, in_specs=[vmem, vmem], out_specs=pl.BlockSpe...  3.51 us
    pallas_call x1, Pallas kernels, shards(): pl.pallas_call(early_kernel, in_specs=[smem] + [vmem] * (3 + len(pairs)),...  2.47 us
    ppermute x1, starting transfers between devices, shards(): out1 = lax.ppermute(own, row, outward)  2.05 us
  transfers between devices with their start and end apart: 7, of which 1 were waited for; matrix products, arithmetic and copies ran while one was open for 0% of the time, Pallas kernels for 10%

profile of v3, /device:TPU:97, one launch (start us, length us, event | category | flops | bytes accessed | tf_op | source)
XLA Modules:
  0.0 70.9 jit_solution(2466826872643834125)
XLA Ops:
  0.0 0.0 copy-start
  0.0 1.3 %copy-done = f32[768,384]{1,0:T(8,128)S(1)} copy-done((f32[768,384]{1,0:T(8,128)S(1)}, f32[768,384]{1,0:T(8,128)}, u32[]{:S(2)}) %copy-start) | copy-done | bytes 1179672
  1.3 0.8 %constant_dynamic-slice_fusion.1 = f32[256,384]{1,0:T(8,128)} fusion(f32[768,384]{1,0:T(8,128)S(1)} %copy-done, s32[]{:T(128)S(6)} %select_n.10), kind=kLoop, calls=%fused_computation.1 | loop fusion | bytes 786436 | tf_op jit(solution)/shard_map/dynamic_slice | solution.py:242
  2.0 3.2 %collective-permute-start.2 = (f32[256,384]{1,0:T(8,128)}, f32[256,384]{1,0:T(8,128)S(1)}, u32[]{:S(2)}, u32[]{:S(2)}) collective-permute-start(f32[256,384]{1,0:T(8,128)} %constant_dynamic-slice_fusion.1), channel_id=1, source_target_pairs={{0,16},{16,0},{32,48},{48,32},{64,80},{80,64},{96,112},{112,96},{1... | collective-permute-start | bytes 1179656 | tf_op jit(solution)/shard_map/ppermute | solution.py:244
  5.3 0.0 copy-start.1
  5.3 0.0 copy-start.3
  5.3 2.1 %collective-permute-start = (f32[384,384]{1,0:T(8,128)S(1)}, f32[384,384]{1,0:T(8,128)S(1)}, u32[]{:S(2)}, u32[]{:S(2)}) collective-permute-start(f32[384,384]{1,0:T(8,128)S(1)} %constant_dynamic-slice_fusion.2.refs_0_.own), channel_id=1, source_target_pairs={{16,48},{32,0},{48,80},{64,32},{80,112},{96,64},{112,144},{128,96}... | collective-permute-start | bytes 1769480 | tf_op jit(solution)/shard_map/ppermute | solution.py:247
  7.4 4.9 %collective-permute-start.3 = (f32[128,384]{1,0:T(8,128)S(1)}, f32[128,384]{1,0:T(8,128)S(1)}, u32[]{:S(2)}, u32[]{:S(2)}) collective-permute-start(f32[128,384]{1,0:T(8,128)S(1)} %constant_dynamic-slice_fusion), channel_id=1, source_target_pairs={{0,16},{16,0},{32,48},{48,32},{64,80},{80,64},{96,112},{112,96},{1... | collective-permute-start | bytes 589832 | tf_op jit(solution)/shard_map/ppermute | solution.py:244
  12.3 1.8 %collective-permute-done.2.refs_0_ = f32[256,384]{1,0:T(8,128)S(1)} collective-permute-done((f32[256,384]{1,0:T(8,128)}, f32[256,384]{1,0:T(8,128)S(1)}, u32[]{:S(2)}, u32[]{:S(2)}) %collective-permute-start.2) | collective-permute-done | bytes 393248 | tf_op jit(solution)/shard_map/ppermute | solution.py:244
  14.1 4.7 %collective-permute-start.6 = (f32[256,384]{1,0:T(8,128)S(1)}, f32[256,384]{1,0:T(8,128)}, u32[]{:S(2)}, u32[]{:S(2)}) collective-permute-start(f32[256,384]{1,0:T(8,128)S(1)} %collective-permute-done.2.refs_0_), channel_id=1, source_target_pairs={{48,16},{0,32},{80,48},{32,64},{112,80},{64,96},{144,112},{96,128}... | collective-permute-start | bytes 1179656 | tf_op jit(solution)/shard_map/ppermute | solution.py:245
  18.9 0.0 copy-start.2
  18.9 0.1 pad_add_fusion.place_ref
  19.0 0.6 pick.2
  19.5 3.5 %collective-permute-start.1 = (f32[384,128]{1,0:T(8,128)S(1)}, f32[384,128]{1,0:T(8,128)S(1)}, u32[]{:S(2)}, u32[]{:S(2)}) collective-permute-start(f32[384,128]{1,0:T(8,128)S(1)} %pick.2), channel_id=1, source_target_pairs={{48,16},{0,32},{80,48},{32,64},{112,80},{64,96},{144,112},{96,128}... | collective-permute-start | bytes 589832 | tf_op jit(solution)/shard_map/ppermute | solution.py:246
  23.1 0.0 collective-permute-done.3.refs_1_
  23.1 0.6 pick.3
  23.7 1.9 %collective-permute-start.4 = (f32[384,128]{1,0:T(8,128)S(1)}, f32[384,128]{1,0:T(8,128)S(1)}, u32[]{:S(2)}, u32[]{:S(2)}) collective-permute-start(f32[384,128]{1,0:T(8,128)S(1)} %pick.3), channel_id=1, source_target_pairs={{16,48},{32,0},{48,80},{64,32},{80,112},{96,64},{112,144},{128,96}... | collective-permute-start | bytes 589832 | tf_op jit(solution)/shard_map/ppermute | solution.py:248
  25.6 4.6 %collective-permute-start.5 = (f32[128,384]{1,0:T(8,128)S(1)}, f32[128,384]{1,0:T(8,128)S(1)}, u32[]{:S(2)}, u32[]{:S(2)}) collective-permute-start(f32[128,384]{1,0:T(8,128)S(1)} %collective-permute-done.3.refs_1_), channel_id=1, source_target_pairs={{48,16},{0,32},{80,48},{32,64},{112,80},{64,96},{144,112},{96,128}... | collective-permute-start | bytes 589832 | tf_op jit(solution)/shard_map/ppermute | solution.py:245
  30.2 0.0 copy-done.1
  30.2 0.0 copy-done.3
  30.2 0.0 copy-done.2
  30.2 0.9 %coefs.1 = f32[4,832,128]{2,1,0:T(8,128)S(1)} custom-call(s32[4]{0:T(128)S(1)} %copy-done.3, f32[8,96,128]{2,1,0:T(8,128)S(1)} %copy-done.1, f32[8,96,128]{2,1,0:T(8,128)S(1)} %copy-done.2), custom_call_target="tpu_custom_call" | custom-call | tf_op jit(solution)/shard_map/coefs/pallas_call | solution.py:45
  31.2 0.0 collective-permute-done.out1
  31.2 2.5 %early.1 = (f32[15,384,128]{2,1,0:T(8,128)S(1)}, f32[128,384]{1,0:T(8,128)S(1)}) custom-call(s32[2]{0:T(128)S(1)} %pad_add_fusion.place_ref, f32[4,104,8,128]{3,2,1,0:T(8,128)S(1)} %bitcast.4, f32[384,384]{1,0:T(8,128)S(1)} %constant_dynamic-slice_fusion.2.refs_0_.own, f32[384,384]{1,0:T(8,128)S(1)} %collective-permute-done.out1, ...), custom_call_target="tpu_custom_call" | custom-call | tf_op jit(solution)/shard_map/early/pallas_call | solution.py:252
  33.7 0.0 collective-permute-done.1.in1
  33.7 0.0 collective-permute-done.4.out2
  33.7 0.0 collective-permute-done.6.in2
  33.7 2.7 %shard_map.46.refs_0_ = f32[768,256]{1,0:T(8,128)S(1)} custom-call(s32[2]{0:T(128)S(1)} %pad_add_fusion.place_ref, f32[4,104,8,128]{3,2,1,0:T(8,128)S(1)} %bitcast.5, f32[384,384]{1,0:T(8,128)S(1)} %constant_dynamic-slice_fusion.2.refs_0_.own, f32[384,384]{1,0:T(8,128)S(1)} %collective-permute-done.out1, f32[384,128]{1,0:T(8,128)S(1)} %collective-permute-done.1.in1, ...), custom_call_target="tpu_custom_call" | custom-call | tf_op jit(solution)/shard_map/pallas_call | solution.py:264
  36.4 0.0 collective-permute-done.5.in2
  36.4 1.5 %shard_map.47 = f32[768,384]{1,0:T(8,128)S(1)} custom-call(s32[2]{0:T(128)S(1)} %pad_add_fusion.place_ref, f32[4,104,8,128]{3,2,1,0:T(8,128)S(1)} %bitcast.6, f32[384,384]{1,0:T(8,128)S(1)} %constant_dynamic-slice_fusion.2.refs_0_.own, f32[384,384]{1,0:T(8,128)S(1)} %collective-permute-done.out1, f32[384,128]{1,0:T(8,128)S(1)} %collective-permute-done.1.in1, ...), custom_call_target="tpu_custom_call" | custom-call | tf_op jit(solution)/shard_map/pallas_call | solution.py:264
  38.0 29.4 %all_to_all.5.got_ref = f32[32,24,384]{2,1,0:T(8,128)S(1)} all-to-all(f32[32,24,384]{2,1,0:T(8,128)S(1)} %bitcast.8), channel_id=1, replica_groups=mesh['z'=16,'yl'=2,'x'=4,'yh'=2,'core'=2] {'yl','x','yh','core'}, dimensions={0} | all-to-all | bytes 2359296 | tf_op jit(solution)/shard_map/all_to_all | solution.py:279
  67.4 3.5 %right.1 = f32[24,12288]{1,0:T(8,128)} custom-call(f32[4,104,8,128]{3,2,1,0:T(8,128)S(1)} %bitcast.7, f32[32,24,384]{2,1,0:T(8,128)S(1)} %all_to_all.5.got_ref), custom_call_target="tpu_custom_call" | custom-call | tf_op jit(solution)/shard_map/right/pallas_call | solution.py:282
  (2 shorter events, 0.1 us)
Async XLA Ops:
  0.0 1.3 %copy-start = (f32[768,384]{1,0:T(8,128)S(1)}, f32[768,384]{1,0:T(8,128)}, u32[]{:S(2)}) copy-start(f32[768,384]{1,0:T(8,128)} %param.4) | copy-start | bytes 3538948
  2.0 12.1 %collective-permute-start.2 = (f32[256,384]{1,0:T(8,128)}, f32[256,384]{1,0:T(8,128)S(1)}, u32[]{:S(2)}, u32[]{:S(2)}) collective-permute-start(f32[256,384]{1,0:T(8,128)} %constant_dynamic-slice_fusion.1), channel_id=1, source_target_pairs={{0,16},{16,0},{32,48},{48,32},{64,80},{80,64},{96,112},{112,96},{1... | collective-permute-start | bytes 1179656 | tf_op jit(solution)/shard_map/ppermute | solution.py:244
  5.3 24.9 %copy-start.1 = (f32[8,96,128]{2,1,0:T(8,128)S(1)}, f32[8,96,128]{2,1,0:T(8,128)}, u32[]{:S(2)}) copy-start(f32[8,96,128]{2,1,0:T(8,128)} %cx_ref.1) | copy-start | bytes 1179652
  5.3 24.9 %copy-start.3 = (s32[4]{0:T(128)S(1)}, s32[4]{0:T(128)}, u32[]{:S(2)}) copy-start(s32[4]{0:T(128)} %wind_ref.1) | copy-start | bytes 52
  5.3 25.8 %collective-permute-start = (f32[384,384]{1,0:T(8,128)S(1)}, f32[384,384]{1,0:T(8,128)S(1)}, u32[]{:S(2)}, u32[]{:S(2)}) collective-permute-start(f32[384,384]{1,0:T(8,128)S(1)} %constant_dynamic-slice_fusion.2.refs_0_.own), channel_id=1, source_target_pairs={{16,48},{32,0},{48,80},{64,32},{80,112},{96,64},{112,144},{128,96}... | collective-permute-start | bytes 1769480 | tf_op jit(solution)/shard_map/ppermute | solution.py:247
  7.4 15.7 %collective-permute-start.3 = (f32[128,384]{1,0:T(8,128)S(1)}, f32[128,384]{1,0:T(8,128)S(1)}, u32[]{:S(2)}, u32[]{:S(2)}) collective-permute-start(f32[128,384]{1,0:T(8,128)S(1)} %constant_dynamic-slice_fusion), channel_id=1, source_target_pairs={{0,16},{16,0},{32,48},{48,32},{64,80},{80,64},{96,112},{112,96},{1... | collective-permute-start | bytes 589832 | tf_op jit(solution)/shard_map/ppermute | solution.py:244
  14.1 19.5 %collective-permute-start.6 = (f32[256,384]{1,0:T(8,128)S(1)}, f32[256,384]{1,0:T(8,128)}, u32[]{:S(2)}, u32[]{:S(2)}) collective-permute-start(f32[256,384]{1,0:T(8,128)S(1)} %collective-permute-done.2.refs_0_), channel_id=1, source_target_pairs={{48,16},{0,32},{80,48},{32,64},{112,80},{64,96},{144,112},{96,128}... | collective-permute-start | bytes 1179656 | tf_op jit(solution)/shard_map/ppermute | solution.py:245
  18.9 11.3 %copy-start.2 = (f32[8,96,128]{2,1,0:T(8,128)S(1)}, f32[8,96,128]{2,1,0:T(8,128)}, u32[]{:S(2)}) copy-start(f32[8,96,128]{2,1,0:T(8,128)} %cy_ref.1) | copy-start | bytes 1179652
  19.5 14.1 %collective-permute-start.1 = (f32[384,128]{1,0:T(8,128)S(1)}, f32[384,128]{1,0:T(8,128)S(1)}, u32[]{:S(2)}, u32[]{:S(2)}) collective-permute-start(f32[384,128]{1,0:T(8,128)S(1)} %pick.2), channel_id=1, source_target_pairs={{48,16},{0,32},{80,48},{32,64},{112,80},{64,96},{144,112},{96,128}... | collective-permute-start | bytes 589832 | tf_op jit(solution)/shard_map/ppermute | solution.py:246
  23.7 10.0 %collective-permute-start.4 = (f32[384,128]{1,0:T(8,128)S(1)}, f32[384,128]{1,0:T(8,128)S(1)}, u32[]{:S(2)}, u32[]{:S(2)}) collective-permute-start(f32[384,128]{1,0:T(8,128)S(1)} %pick.3), channel_id=1, source_target_pairs={{16,48},{32,0},{48,80},{64,32},{80,112},{96,64},{112,144},{128,96}... | collective-permute-start | bytes 589832 | tf_op jit(solution)/shard_map/ppermute | solution.py:248
  25.6 10.8 %collective-permute-start.5 = (f32[128,384]{1,0:T(8,128)S(1)}, f32[128,384]{1,0:T(8,128)S(1)}, u32[]{:S(2)}, u32[]{:S(2)}) collective-permute-start(f32[128,384]{1,0:T(8,128)S(1)} %collective-permute-done.3.refs_1_), channel_id=1, source_target_pairs={{48,16},{0,32},{80,48},{32,64},{112,80},{64,96},{144,112},{96,128}... | collective-permute-start | bytes 589832 | tf_op jit(solution)/shard_map/ppermute | solution.py:245
